TPU v7x, 32 devices: a whole 2x2x4 slice. The times are simulated.
32 devices in a mesh: gx: 8 (over z, y), gy: 4 (over x, core).
Axes of the slice: x: 2, y: 2, z: 4, core: 2. Of those that a mesh axis runs over, the one named last changes fastest.
Arguments:
- positions: float32 [3, 8192, 128], P(None, ('gx', 'gy')), may hold values from 0 to 1
- masses: float32 [8192, 128], P(('gx', 'gy')), may hold values from 0.004 to 0.012
- smoothing: float32 [8192, 128], P(('gx', 'gy')), may hold values from 0.55 to 1
- entropy: float32 [8192, 128], P(('gx', 'gy')), may hold values from 0.5 to 2
- density: float32 [8192, 128], P(('gx', 'gy')), may hold values from 0.5 to 2
- active_cells: int32 [128], P(('gx', 'gy')), may hold values from 0 to 8191, as said below
- active_count: int32 [32], P(('gx', 'gy')), may hold values from 1 to 4, 84 in all
- neighbours: int32 [128, 27], P(('gx', 'gy')), may hold values from 0 to 8191, as said below
- mig_source: int32 [4096], P(('gx', 'gy')), may hold values from 0 to 32767
- mig_dest: int32 [4096, 1], P(('gx', 'gy')), may hold values from 0 to 31; in each aligned block of 128 rows (0 to 127, 128 to 255, ...) at most 8 rows name the same one
Outputs:
- new_density: float32 [8192, 128], P(('gx', 'gy'))
- acceleration: float32 [3, 128, 128], P(None, ('gx', 'gy'))
- arrivals: float32 [7, 8192], P(None, ('gx', 'gy'))
Inputs may be any that keep to these rules, and one draw needn't show every extreme that they name: `active_cells`: the 4 entries of device d are distinct cells of device d. The middle entry (index 13) of a slot is its active cell. Every other entry is a cell of the slot's own device, or a cell of the device just before or just after it in the cell order lying within 64 cells of the end they share. Over all slots of one device, at most 8 distinct cells of each of these two devices are named, and every device with neighbours on both sides names exactly 8 on each side. `mig_dest`: within the 128 rows of one device no destination appears more than 8 times; some destination appears exactly 8 times.
All inputs are finite; a program needn't handle non-finite values. No bound on the sum of `active_count` on one device may be relied on, other than what follows from the above.
Results may differ from a plain program's by a relative error of at most 0.0003.
Values sent between devices are 32-bit elements; how exact they have to be, the bound alone decides.
No kernel may reach another device: no remote copies, remote signals or barrier semaphores. Data moves between devices by JAX's collectives and lax.ppermute only.
A program may use at most 64 MiB of HBM per device.

v0:
```python
import math
import jax
import jax.numpy as jnp
from jax import lax
from jax.sharding import PartitionSpec as P

P_SIZE = 128
NBR = 27
RIM = 64
kernel_norm = 8.0 / math.pi


def padded(block, sides, width):
    for axis, dim in sides:
        count = lax.axis_size(axis)
        forward = [(i, i + 1) for i in range(count - 1)]
        backward = [(target, source) for source, target in forward]
        low = lax.ppermute(
            lax.slice_in_dim(block, block.shape[dim] - width, None, axis=dim), axis, forward
        )
        high = lax.ppermute(lax.slice_in_dim(block, 0, width, axis=dim), axis, backward)
        block = jnp.concatenate([low, block, high], axis=dim)
    return block


def stencil_offsets():
    index = jnp.arange(NBR)
    return jnp.stack([index // 9 - 1, index // 3 % 3 - 1, index % 3 - 1]).astype(jnp.float32)


def kernel_value(ratio):
    inner = 1.0 - 6.0 * ratio * ratio + 6.0 * ratio * ratio * ratio
    outer = 2.0 * (1.0 - ratio) ** 3
    return jnp.where(ratio < 0.5, inner, jnp.where(ratio < 1.0, outer, 0.0))


def kernel_slope(ratio):
    safe_ratio = jnp.maximum(ratio, 0.5)
    inner = -12.0 + 18.0 * ratio
    outer = -6.0 * (1.0 - ratio) ** 2 / safe_ratio
    return jnp.where(ratio < 0.5, inner, jnp.where(ratio < 1.0, outer, 0.0))


def pair_geometry(own_pos, other_pos):
    separation = own_pos[:, :, None, None] - other_pos[:, None, :, :]
    distance = jnp.sqrt(jnp.sum(separation * separation, axis=0))
    return (separation, distance)


def density_cell(own_pos, own_len, other_pos, other_mass):
    separation, distance = pair_geometry(own_pos, other_pos)
    weights = kernel_value(distance / own_len[:, None, None])
    return kernel_norm * jnp.sum(other_mass[None] * weights, axis=(1, 2)) / own_len**3


def force_cell(
    own_pos, own_len, own_rho, own_press, other_pos, other_mass, other_len, other_rho, other_press
):
    separation, distance = pair_geometry(own_pos, other_pos)
    own_term = (own_press / own_rho**2 * kernel_norm / own_len**5)[
        :, None, None
    ] * kernel_slope(distance / own_len[:, None, None])
    other_term = (other_press / other_rho**2 * kernel_norm / other_len**5)[None] * kernel_slope(
        distance / other_len[None]
    )
    factor = other_mass[None] * (own_term + other_term)
    return -jnp.sum(factor[None] * separation, axis=(2, 3))


def gather_slots(table_pos, lookup_ids, stencil):
    near_pos = jnp.take(table_pos, lookup_ids, axis=1) + stencil[:, None, :, None]
    return jnp.moveaxis(near_pos, 1, 0)


def local(
    positions,
    masses,
    smoothing,
    entropy,
    density,
    active_cells,
    active_count,
    neighbours,
    mig_source,
    mig_dest,
):
    cell_count = masses.shape[0]
    slot_count = active_cells.shape[0]
    my_index = lax.axis_index(("gx", "gy"))
    devices = lax.axis_size(("gx", "gy"))
    stencil = stencil_offsets()
    local_active = active_cells - my_index * cell_count
    near_index = neighbours - (my_index * cell_count - RIM)
    live_slot = jnp.arange(slot_count) < active_count[0]
    first_rows = jnp.concatenate([positions, masses[None]], axis=0)
    extended = padded(first_rows, ((("gx", "gy"), 1),), RIM)
    own_pos = jnp.moveaxis(jnp.take(positions, local_active, axis=1), 1, 0)
    own_len = smoothing[local_active]
    near_pos = gather_slots(extended[0:3], near_index, stencil)
    near_mass = extended[3][near_index]

    def density_one(inputs):
        cell_pos, cell_len, other_pos, other_mass = inputs
        return density_cell(cell_pos, cell_len, other_pos, other_mass)

    rho = lax.map(density_one, (own_pos, own_len, near_pos, near_mass))
    kept = jnp.where(live_slot[:, None], rho, density[local_active])
    new_density = density.at[local_active].set(kept)
    pressure = entropy * jnp.exp(5.0 / 3.0 * jnp.log(new_density))
    state_rows = jnp.concatenate(
        [positions, masses[None], smoothing[None], new_density[None], pressure[None]], axis=0
    )
    ghost_all = padded(state_rows, ((("gx", "gy"), 1),), RIM)
    force_pos = gather_slots(ghost_all[0:3], near_index, stencil)
    force_mass = ghost_all[3][near_index]
    force_len = ghost_all[4][near_index]
    force_rho = ghost_all[5][near_index]
    force_press = ghost_all[6][near_index]
    own_rho = new_density[local_active]
    own_press = pressure[local_active]

    def force_one(inputs):
        (
            cell_pos,
            cell_len,
            cell_rho,
            cell_press,
            other_pos,
            other_mass,
            other_len,
            other_rho,
            other_press,
        ) = inputs
        return force_cell(
            cell_pos,
            cell_len,
            cell_rho,
            cell_press,
            other_pos,
            other_mass,
            other_len,
            other_rho,
            other_press,
        )

    accel_rows = lax.map(
        force_one,
        (
            own_pos,
            own_len,
            own_rho,
            own_press,
            force_pos,
            force_mass,
            force_len,
            force_rho,
            force_press,
        ),
    )
    acceleration = jnp.transpose(accel_rows, (1, 0, 2)) * live_slot[None, :, None].astype(
        jnp.float32
    )
    mig_rows = mig_source.shape[0]
    capacity = max(2, 2 * mig_rows // devices)
    flat_count = cell_count * P_SIZE
    payload = jnp.concatenate(
        [
            positions.reshape(3, flat_count)[:, mig_source],
            masses.reshape(flat_count)[mig_source][None],
            smoothing.reshape(flat_count)[mig_source][None],
            entropy.reshape(flat_count)[mig_source][None],
            new_density.reshape(flat_count)[mig_source][None],
        ],
        axis=0,
    )
    destination = mig_dest[:, 0]
    same = destination[:, None] == destination[None, :]
    earlier = jnp.arange(mig_rows)[None, :] < jnp.arange(mig_rows)[:, None]
    slot_rank = jnp.sum(jnp.logical_and(same, earlier), axis=1)
    column = destination * capacity + slot_rank
    outgoing = jnp.zeros((7, devices * capacity), jnp.float32).at[:, column].set(payload)
    arrivals = lax.all_to_all(outgoing, ("gx", "gy"), split_axis=1, concat_axis=1, tiled=True)
    return (new_density, acceleration, arrivals)


def solution(mesh):
    placed = (
        P(None, ("gx", "gy"), None),
        P(("gx", "gy"), None),
        P(("gx", "gy"), None),
        P(("gx", "gy"), None),
        P(("gx", "gy"), None),
        P(("gx", "gy")),
        P(("gx", "gy")),
        P(("gx", "gy"), None),
        P(("gx", "gy")),
        P(("gx", "gy"), None),
    )
    return jax.shard_map(
        local,
        mesh=mesh,
        in_specs=placed,
        out_specs=(P(("gx", "gy"), None), P(None, ("gx", "gy"), None), P(None, ("gx", "gy"))),
        check_vma=False,
    )
```

profile of v0, /device:TPU:0, one launch (start us, length us, event | category | flops | bytes accessed | tf_op | source)
XLA Modules:
  0.0 87.4 jit_solution(12953888744872572733)
XLA Ops:
  0.7 1.1 %pad_maximum_fusion.5 = (f32[4,64,128]{2,1,0:T(8,128)S(1)}, f32[4,64,128]{2,1,0:T(8,128)S(1)}) fusion(f32[1,256,128]{2,1,0:T(8,128)} %bitcast.109, f32[3,256,128]{2,1,0:T(8,128)} %param.16), kind=kLoop, calls=%fused_computation.73 | loop fusion | flops 65536 | bytes 786432 | tf_op jit(solution)/shard_map/slice | solution.py:19
  1.8 2.4 %collective-permute-start = (f32[4,64,128]{2,1,0:T(8,128)S(1)}, f32[4,64,128]{2,1,0:T(8,128)S(1)}, u32[]{:S(2)}, u32[]{:S(2)}) collective-permute-start(f32[4,64,128]{2,1,0:T(8,128)S(1)} %get-tuple-element.197), channel_id=1, source_target_pairs={{0,1},{1,2},{2,3},{3,4},{4,5},{5,6},{6,7},{7,8},{8,9},{9,10},{10,1... | collective-permute-start | bytes 393224 | tf_op jit(solution)/shard_map/ppermute | solution.py:18
  4.2 1.3 %collective-permute-start.1 = (f32[4,64,128]{2,1,0:T(8,128)S(1)}, f32[4,64,128]{2,1,0:T(8,128)S(1)}, u32[]{:S(2)}, u32[]{:S(2)}) collective-permute-start(f32[4,64,128]{2,1,0:T(8,128)S(1)} %get-tuple-element.198), channel_id=1, source_target_pairs={{1,0},{2,1},{3,2},{4,3},{5,4},{6,5},{7,6},{8,7},{9,8},{10,9},{11,1... | collective-permute-start | bytes 393224 | tf_op jit(solution)/shard_map/ppermute | solution.py:21
  5.5 1.0 %constant_dynamic-update-slice_fusion.1 = f32[7,256,128]{2,1,0:T(8,128)S(1)} fusion(f32[3,256,128]{2,1,0:T(8,128)} %param.16), kind=kLoop, calls=%fused_computation.84 | loop fusion | bytes 786432
  8.7 8.7 %copy.60 = f32[3,256,128]{0,2,1:T(8,128)} copy(f32[3,256,128]{2,1,0:T(8,128)S(1)} %copy-done) | data formatting | bytes 786432 | tf_op args[0]
  17.4 6.4 %gather_fusion.9 = f32[128,3]{1,0:T(8,128)S(1)} fusion(f32[3,32768]{0,1:T(8,128)} %bitcast.107, s32[1024]{0:T(1024)S(1)} %pad_clamp_fusion), kind=kCustom, calls=%fused_computation.12 | custom fusion | bytes 3584 | tf_op jit(solution)/shard_map/gather | solution.py:168
  23.9 1.2 %gather_fusion.10 = f32[128]{0:T(128)S(1)} fusion(f32[32768]{0:T(1024)S(1)} %bitcast.110, s32[1024]{0:T(1024)S(1)} %pad_clamp_fusion), kind=kCustom, calls=%fused_computation.13 | custom fusion | bytes 1536 | tf_op jit(solution)/shard_map/gather | solution.py:169
  25.0 1.1 %gather_fusion.11 = f32[128]{0:T(128)S(1)} fusion(f32[32768]{0:T(1024)S(1)} %bitcast.113, s32[1024]{0:T(1024)S(1)} %pad_clamp_fusion), kind=kCustom, calls=%fused_computation.14 | custom fusion | bytes 1536 | tf_op jit(solution)/shard_map/gather | solution.py:170
  26.2 1.1 %gather_fusion.12 = f32[128]{0:T(128)S(1)} fusion(f32[32768]{0:T(1024)S(1)} %bitcast.114, s32[1024]{0:T(1024)S(1)} %pad_clamp_fusion), kind=kCustom, calls=%fused_computation.15 | custom fusion | bytes 1536 | tf_op jit(solution)/shard_map/gather | solution.py:171
  28.0 0.7 gather_fusion.14
  28.8 0.6 gather_fusion
  29.5 9.0 %while.20 = (s32[]{:T(128)}, f32[4,128]{1,0:T(4,128)S(1)}, f32[4,27,128]{2,1,0:T(8,128)S(1)}, f32[4,3,128]{2,1,0:T(4,128)S(1)}, f32[4,3,27,128]{3,2,0,1:T(8,128)...) while((s32[]{:T(128)}, f32[4,128]{1,0:T(4,128)S(1)}, f32[4,27,128]{2,1,0:T(8,128)S(1)}, ...), condition=%wide.region_3.5_spmd, body=%wide.region_0.4_spmd.sunk | while | flops 10617218 | bytes 3714157 | solution.py:106
  29.6 0.7 multiply_reduce_fusion.2
  30.3 1.4 %fusion.40 = f32[128]{0:T(128)S(1)} fusion(f32[128,27,128]{2,0,1:T(8,128)S(1)} %multiply_reduce_fusion.2, f32[128]{0:T(128)S(1)} %fusion.39, f32[27,128]{1,0:T(8,128)S(1)} %dynamic-slice_bitcast_fusion.12), kind=kLoop, calls=%fused_computation.27.clone.1 | loop fusion | flops 7077760 | bytes 1784320 | tf_op jit(solution)/shard_map/while/body/eval_jaxpr/reduce_sum | solution.py:53
  31.8 0.7 multiply_reduce_fusion.2
  32.6 1.4 %fusion.40 = f32[128]{0:T(128)S(1)} fusion(f32[128,27,128]{2,0,1:T(8,128)S(1)} %multiply_reduce_fusion.2, f32[128]{0:T(128)S(1)} %fusion.39, f32[27,128]{1,0:T(8,128)S(1)} %dynamic-slice_bitcast_fusion.12), kind=kLoop, calls=%fused_computation.27.clone.1 | loop fusion | flops 7077760 | bytes 1784320 | tf_op jit(solution)/shard_map/while/body/eval_jaxpr/reduce_sum | solution.py:53
  34.1 0.7 multiply_reduce_fusion.2
  34.8 1.4 %fusion.40 = f32[128]{0:T(128)S(1)} fusion(f32[128,27,128]{2,0,1:T(8,128)S(1)} %multiply_reduce_fusion.2, f32[128]{0:T(128)S(1)} %fusion.39, f32[27,128]{1,0:T(8,128)S(1)} %dynamic-slice_bitcast_fusion.12), kind=kLoop, calls=%fused_computation.27.clone.1 | loop fusion | flops 7077760 | bytes 1784320 | tf_op jit(solution)/shard_map/while/body/eval_jaxpr/reduce_sum | solution.py:53
  36.4 0.7 multiply_reduce_fusion.2
  37.1 1.4 %fusion.40 = f32[128]{0:T(128)S(1)} fusion(f32[128,27,128]{2,0,1:T(8,128)S(1)} %multiply_reduce_fusion.2, f32[128]{0:T(128)S(1)} %fusion.39, f32[27,128]{1,0:T(8,128)S(1)} %dynamic-slice_bitcast_fusion.12), kind=kLoop, calls=%fused_computation.27.clone.1 | loop fusion | flops 7077760 | bytes 1784320 | tf_op jit(solution)/shard_map/while/body/eval_jaxpr/reduce_sum | solution.py:53
  38.6 0.7 scatter_custom_fusion
  39.4 5.1 %collective-permute-start.2 = (f32[7,64,128]{2,1,0:T(8,128)S(1)}, f32[7,64,128]{2,1,0:T(8,128)S(1)}, u32[]{:S(2)}, u32[]{:S(2)}) collective-permute-start(f32[7,64,128]{2,1,0:T(8,128)S(1)} %get-tuple-element.195), channel_id=1, source_target_pairs={{0,1},{1,2},{2,3},{3,4},{4,5},{5,6},{6,7},{7,8},{8,9},{9,10},{10,1... | collective-permute-start | bytes 688136 | tf_op jit(solution)/shard_map/ppermute | solution.py:18
  44.6 1.3 %collective-permute-start.3 = (f32[7,64,128]{2,1,0:T(8,128)S(1)}, f32[7,64,128]{2,1,0:T(8,128)S(1)}, u32[]{:S(2)}, u32[]{:S(2)}) collective-permute-start(f32[7,64,128]{2,1,0:T(8,128)S(1)} %get-tuple-element.196), channel_id=1, source_target_pairs={{1,0},{2,1},{3,2},{4,3},{5,4},{6,5},{7,6},{8,7},{9,8},{10,9},{11,1... | collective-permute-start | bytes 688136 | tf_op jit(solution)/shard_map/ppermute | solution.py:21
  45.9 1.1 %gather_fusion.13 = f32[128]{0:T(128)S(1)} fusion(f32[32768]{0:T(1024)S(1)} %bitcast.108, s32[1024]{0:T(1024)S(1)} %pad_clamp_fusion), kind=kCustom, calls=%fused_computation.16 | custom fusion | bytes 1536 | tf_op jit(solution)/shard_map/gather | solution.py:172
  47.2 0.9 %scatter_custom_fusion.1 = f32[7,256]{0,1:T(8,128)S(1)} fusion(s32[128]{0:T(128)S(1)} %fusion.28, f32[128,7]{1,0:T(8,128)S(1)} %copy.62, f32[]{:T(128)} %constant.137.clone.1), kind=kCustom, calls=%fused_computation.80 | custom fusion | bytes 7172 | tf_op jit(solution)/shard_map/scatter | solution.py:181
  48.1 0.9 %copy.63 = f32[7,32,8]{2,0,1:T(8,128)} copy(f32[7,32,8]{0,2,1:T(8,128)S(1)} %bitcast.117) | data formatting | bytes 14336 | tf_op jit(solution)/shard_map/all_to_all | solution.py:182
  49.0 10.0 %all-to-all-start = ((f32[7,32,8]{2,0,1:T(8,128)}), f32[7,32,8]{2,0,1:T(8,128)S(1)}, u32[]{:S(2)}, u32[]{:S(2)}) async-start(f32[7,32,8]{2,0,1:T(8,128)} %copy.63), calls=%async_computation | async-start | bytes 262144 | tf_op jit(solution)/shard_map/all_to_all | solution.py:182
  60.2 7.1 %all-to-all-done = f32[7,32,8]{2,0,1:T(8,128)S(1)} async-done(((f32[7,32,8]{2,0,1:T(8,128)}), f32[7,32,8]{2,0,1:T(8,128)S(1)}, u32[]{:S(2)}, u32[]{:S(2)}) %all-to-all-start) | async-done | bytes 7200 | tf_op jit(solution)/shard_map/all_to_all | solution.py:182
  67.3 0.7 all_to_all.10
  68.6 0.7 gather_fusion.15
  69.5 0.6 gather_fusion.6
  70.1 0.6 gather_fusion.7
  70.8 0.6 gather_fusion.8
  71.4 0.6 gather_fusion.3
  72.0 14.6 %while.21 = (s32[]{:T(128)}, f32[4,3,128]{2,0,1:T(4,128)S(1)}, f32[4,27,128]{2,1,0:T(8,128)S(1)}, f32[4,128]{1,0:T(4,128)S(1)}, f32[4,128]{1,0:T(4,128)S(1)}, /*...) while((s32[]{:T(128)}, f32[4,3,128]{2,0,1:T(4,128)S(1)}, ...), condition=%wide.region_8.10_spmd, body=%wide.region_5.9_spmd.sunk | while | flops 19931648 | bytes 7402641 | solution.py:146
  72.1 0.7 fusion.43
  72.8 2.1 %add_multiply_fusion.2 = f32[128,27,128]{2,0,1:T(8,128)S(1)} fusion(f32[128,27,128]{2,0,1:T(8,128)S(1)} %fusion.43, f32[27,128]{1,0:T(8,128)S(1)} %get-tuple-element.312, f32[27,128]{1,0:T(8,128)S(1)} %get-tuple-element.313, f32[128]{0:T(128)S(1)} %get-tuple-element.314, f32[128]{0:T(128)S(1)} %get-tuple-element.315, f32[27,128]{1,0:T(8,128)S(1)} %get-tuple-element.316), kind=kLoop, calls=%fused_computation.42.clone.1 | loop fusion | flops 12386304 | bytes 3581440 | tf_op jit(solution)/shard_map/while/body/eval_jaxpr/mul | solution.py:66
  75.0 0.7 fusion.44
  75.8 0.7 fusion.43
  76.5 2.1 %add_multiply_fusion.2 = f32[128,27,128]{2,0,1:T(8,128)S(1)} fusion(f32[128,27,128]{2,0,1:T(8,128)S(1)} %fusion.43, f32[27,128]{1,0:T(8,128)S(1)} %get-tuple-element.312, f32[27,128]{1,0:T(8,128)S(1)} %get-tuple-element.313, f32[128]{0:T(128)S(1)} %get-tuple-element.314, f32[128]{0:T(128)S(1)} %get-tuple-element.315, f32[27,128]{1,0:T(8,128)S(1)} %get-tuple-element.316), kind=kLoop, calls=%fused_computation.42.clone.1 | loop fusion | flops 12386304 | bytes 3581440 | tf_op jit(solution)/shard_map/while/body/eval_jaxpr/mul | solution.py:66
  78.6 0.7 fusion.44
  79.4 0.7 fusion.43
  80.1 2.1 %add_multiply_fusion.2 = f32[128,27,128]{2,0,1:T(8,128)S(1)} fusion(f32[128,27,128]{2,0,1:T(8,128)S(1)} %fusion.43, f32[27,128]{1,0:T(8,128)S(1)} %get-tuple-element.312, f32[27,128]{1,0:T(8,128)S(1)} %get-tuple-element.313, f32[128]{0:T(128)S(1)} %get-tuple-element.314, f32[128]{0:T(128)S(1)} %get-tuple-element.315, f32[27,128]{1,0:T(8,128)S(1)} %get-tuple-element.316), kind=kLoop, calls=%fused_computation.42.clone.1 | loop fusion | flops 12386304 | bytes 3581440 | tf_op jit(solution)/shard_map/while/body/eval_jaxpr/mul | solution.py:66
  82.3 0.7 fusion.44
  83.1 0.7 fusion.43
  83.8 2.1 %add_multiply_fusion.2 = f32[128,27,128]{2,0,1:T(8,128)S(1)} fusion(f32[128,27,128]{2,0,1:T(8,128)S(1)} %fusion.43, f32[27,128]{1,0:T(8,128)S(1)} %get-tuple-element.312, f32[27,128]{1,0:T(8,128)S(1)} %get-tuple-element.313, f32[128]{0:T(128)S(1)} %get-tuple-element.314, f32[128]{0:T(128)S(1)} %get-tuple-element.315, f32[27,128]{1,0:T(8,128)S(1)} %get-tuple-element.316), kind=kLoop, calls=%fused_computation.42.clone.1 | loop fusion | flops 12386304 | bytes 3581440 | tf_op jit(solution)/shard_map/while/body/eval_jaxpr/mul | solution.py:66
  85.9 0.7 fusion.44
  86.7 0.7 multiply_bitcast_fusion
  (120 shorter events, 5.2 us)
Async XLA Ops:
  0.6 6.1 %copy-start = (f32[3,256,128]{2,1,0:T(8,128)S(1)}, f32[3,256,128]{2,1,0:T(8,128)}, u32[]{:S(2)}) copy-start(f32[3,256,128]{2,1,0:T(8,128)} %param.16) | copy-start | bytes 1179652
  0.6 7.3 %copy-start.3 = (f32[256,128]{1,0:T(8,128)S(1)}, f32[256,128]{1,0:T(8,128)}, u32[]{:S(2)}) copy-start(f32[256,128]{1,0:T(8,128)} %param.17) | copy-start | bytes 393220
  0.7 7.4 %copy-start.4 = (f32[256,128]{1,0:T(8,128)S(1)}, f32[256,128]{1,0:T(8,128)}, u32[]{:S(2)}) copy-start(f32[256,128]{1,0:T(8,128)} %param.18) | copy-start | bytes 393220
  0.7 5.9 %copy-start.7 = (s32[4]{0:T(128)S(1)}, s32[4]{0:T(128)}, u32[]{:S(2)}) copy-start(s32[4]{0:T(128)} %param.21) | copy-start | bytes 52
  0.7 5.9 %copy-start.6 = (s32[4,27]{1,0:T(4,128)S(1)}, s32[4,27]{1,0:T(4,128)}, u32[]{:S(2)}) copy-start(s32[4,27]{1,0:T(4,128)} %param.23) | copy-start | bytes 1300
  0.7 7.3 %copy-start.8 = (s32[128]{0:T(128)S(1)}, s32[128]{0:T(128)}, u32[]{:S(2)}) copy-start(s32[128]{0:T(128)} %param.24) | copy-start | bytes 1540
  1.8 25.8 %collective-permute-start = (f32[4,64,128]{2,1,0:T(8,128)S(1)}, f32[4,64,128]{2,1,0:T(8,128)S(1)}, u32[]{:S(2)}, u32[]{:S(2)}) collective-permute-start(f32[4,64,128]{2,1,0:T(8,128)S(1)} %get-tuple-element.197), channel_id=1, source_target_pairs={{0,1},{1,2},{2,3},{3,4},{4,5},{5,6},{6,7},{7,8},{8,9},{9,10},{10,1... | collective-permute-start | bytes 393224 | tf_op jit(solution)/shard_map/ppermute | solution.py:18
  4.2 23.4 %collective-permute-start.1 = (f32[4,64,128]{2,1,0:T(8,128)S(1)}, f32[4,64,128]{2,1,0:T(8,128)S(1)}, u32[]{:S(2)}, u32[]{:S(2)}) collective-permute-start(f32[4,64,128]{2,1,0:T(8,128)S(1)} %get-tuple-element.198), channel_id=1, source_target_pairs={{1,0},{2,1},{3,2},{4,3},{5,4},{6,5},{7,6},{8,7},{9,8},{10,9},{11,1... | collective-permute-start | bytes 393224 | tf_op jit(solution)/shard_map/ppermute | solution.py:21
  8.7 17.5 %copy-start.5 = (f32[256,128]{1,0:T(8,128)S(1)}, f32[256,128]{1,0:T(8,128)}, u32[]{:S(2)}) copy-start(f32[256,128]{1,0:T(8,128)} %param.19) | copy-start | bytes 393220
  8.7 18.7 %copy-start.9 = (s32[128,1]{0,1:T(1,128)S(1)}, s32[128,1]{0,1:T(1,128)}, u32[]{:S(2)}) copy-start(s32[128,1]{0,1:T(1,128)} %param.25) | copy-start | bytes 1540
  29.5 9.0 %copy-start.2 = (f32[256,128]{1,0:T(8,128)S(1)}, f32[256,128]{1,0:T(8,128)}, u32[]{:S(2)}) copy-start(f32[256,128]{1,0:T(8,128)} %param.20) | copy-start | bytes 393220
  39.3 28.8 %copy-start.1 = (f32[256,128]{1,0:T(8,128)}, f32[256,128]{1,0:T(8,128)S(1)}, u32[]{:S(2)}) copy-start(f32[256,128]{1,0:T(8,128)S(1)} %scatter_custom_fusion) | copy-start | bytes 393220
  39.4 28.6 %collective-permute-start.2 = (f32[7,64,128]{2,1,0:T(8,128)S(1)}, f32[7,64,128]{2,1,0:T(8,128)S(1)}, u32[]{:S(2)}, u32[]{:S(2)}) collective-permute-start(f32[7,64,128]{2,1,0:T(8,128)S(1)} %get-tuple-element.195), channel_id=1, source_target_pairs={{0,1},{1,2},{2,3},{3,4},{4,5},{5,6},{6,7},{7,8},{8,9},{9,10},{10,1... | collective-permute-start | bytes 688136 | tf_op jit(solution)/shard_map/ppermute | solution.py:18
  44.6 23.4 %collective-permute-start.3 = (f32[7,64,128]{2,1,0:T(8,128)S(1)}, f32[7,64,128]{2,1,0:T(8,128)S(1)}, u32[]{:S(2)}, u32[]{:S(2)}) collective-permute-start(f32[7,64,128]{2,1,0:T(8,128)S(1)} %get-tuple-element.196), channel_id=1, source_target_pairs={{1,0},{2,1},{3,2},{4,3},{5,4},{6,5},{7,6},{8,7},{9,8},{10,9},{11,1... | collective-permute-start | bytes 688136 | tf_op jit(solution)/shard_map/ppermute | solution.py:21
  49.0 18.3 %all-to-all-start = ((f32[7,32,8]{2,0,1:T(8,128)}), f32[7,32,8]{2,0,1:T(8,128)S(1)}, u32[]{:S(2)}, u32[]{:S(2)}) async-start(f32[7,32,8]{2,0,1:T(8,128)} %copy.63), calls=%async_computation | async-start | bytes 262144 | tf_op jit(solution)/shard_map/all_to_all | solution.py:182
where the time goes:
time: 87.7 us; the launch traced here: 87.4 us
  local copies, waits for them, and re-layouts  32 us (36%)
  other arithmetic  25.9 us (30%)
  starting transfers between devices  20.2 us (23%)
  waiting for transfers between devices  7.07 us (8%)
  between operations  1.79 us (2%)
    all_to_all x1, starting transfers between devices, local(): lax.all_to_all(outgoing, ('gx', 'gy'), split_axis=1, concat_axis=1, tiled...  10 us
    unnamed x25, local copies, waits for them, and re-layouts  9.81 us
    mul x4, other arithmetic, force_cell(): factor = other_mass[None] * (own_term + other_term)  8.53 us
    ppermute x2, starting transfers between devices, padded(): lax.ppermute(lax.slice_in_dim(block, block.shape[dim] - width, None, axis...  7.54 us
    all_to_all x1, waiting for transfers between devices, local(): lax.all_to_all(outgoing, ('gx', 'gy'), split_axis=1, concat_axis=1, tiled...  7.06 us
    gather x2, local copies, waits for them, and re-layouts, local(): positions.reshape(3, flat_count)[:, mig_source]  6.47 us
    reduce_sum x4, other arithmetic, density_cell(): jnp.sum(other_mass[None] * weights, axis=(1, 2))  5.79 us
    reduce_sum x8, other arithmetic, pair_geometry(): distance = jnp.sqrt(jnp.sum(separation * separation, axis=0))  5.34 us
  transfers between devices with their start and end apart: 5, of which 1 were waited for; matrix products, arithmetic and copies ran while one was open for 29% of the time, Pallas kernels for 0%

commit v1 on v0

--- a/solution.py
+++ b/solution.py
@@ -179,7 +179,12 @@
     slot_rank = jnp.sum(jnp.logical_and(same, earlier), axis=1)
     column = destination * capacity + slot_rank
     outgoing = jnp.zeros((7, devices * capacity), jnp.float32).at[:, column].set(payload)
-    arrivals = lax.all_to_all(outgoing, ("gx", "gy"), split_axis=1, concat_axis=1, tiled=True)
+    arrivals = jnp.concatenate(
+        lax.all_to_all(
+            jnp.stack(jnp.split(outgoing, lax.axis_size(("gx", "gy")), axis=1)), ("gx", "gy"), 0, 0
+        ),
+        axis=1,
+    )
     return (new_density, acceleration, arrivals)
 
 

time: 87.7 us -> 109 us (1.24)
  local copies, waits for them, and re-layouts: 32 us -> 52.6 us
    unnamed x25 -> x56, local copies, waits for them, and re-layouts: 9.81 us -> 28.1 us
    split x0 -> x34, local copies, waits for them, and re-layouts: none -> 2.6 us  [local(): jnp.split(outgoing, lax.axis_size(('gx', 'gy')), axis=1)]
    all_to_all x3 -> x0, local copies, waits for them, and re-layouts: 1.63 us -> none  [local(): lax.all_to_all(outgoing, ('gx', 'gy'), split_axis=1, concat_axis=1, tiled...]
  transfers between devices with their start and end apart: 5 -> 5, of which waited for: 1 -> 1; matrix products, arithmetic and copies ran while one was open for 29% -> 41% of each run, Pallas kernels for 0% -> 0%
where the time goes in v1:
time: 109 us; the launch traced here: 108 us
  local copies, waits for them, and re-layouts  52.6 us (48%)
  other arithmetic  25.9 us (24%)
  starting transfers between devices  20.7 us (19%)
  waiting for transfers between devices  6.88 us (6%)
  between operations  1.84 us (2%)
    unnamed x56, local copies, waits for them, and re-layouts  28.1 us
    all_to_all x1, starting transfers between devices, local(): lax.all_to_all(jnp.stack(jnp.split(outgoing, lax.axis_size(('gx', 'gy')),...  9.9 us
    mul x4, other arithmetic, force_cell(): factor = other_mass[None] * (own_term + other_term)  8.53 us
    ppermute x2, starting transfers between devices, padded(): lax.ppermute(lax.slice_in_dim(block, block.shape[dim] - width, None, axis...  8.17 us
    all_to_all x1, waiting for transfers between devices, local(): lax.all_to_all(jnp.stack(jnp.split(outgoing, lax.axis_size(('gx', 'gy')),...  6.87 us
    gather x2, local copies, waits for them, and re-layouts, local(): positions.reshape(3, flat_count)[:, mig_source]  6.47 us
    reduce_sum x4, other arithmetic, density_cell(): jnp.sum(other_mass[None] * weights, axis=(1, 2))  5.79 us
    reduce_sum x8, other arithmetic, pair_geometry(): distance = jnp.sqrt(jnp.sum(separation * separation, axis=0))  5.34 us
  transfers between devices with their start and end apart: 5, of which 1 were waited for; matrix products, arithmetic and copies ran while one was open for 41% of the time, Pallas kernels for 0%

profile of v1, /device:TPU:0, one launch (start us, length us, event | category | flops | bytes accessed | tf_op | source)
XLA Modules:
  0.0 108.4 jit_solution(10974316959996240766)
XLA Ops:
  0.7 1.1 %pad_maximum_fusion.5 = (f32[4,64,128]{2,1,0:T(8,128)S(1)}, f32[4,64,128]{2,1,0:T(8,128)S(1)}) fusion(f32[1,256,128]{2,1,0:T(8,128)} %bitcast.173, f32[3,256,128]{2,1,0:T(8,128)} %param.16), kind=kLoop, calls=%fused_computation.73 | loop fusion | flops 65536 | bytes 786432 | tf_op jit(solution)/shard_map/slice | solution.py:19
  1.8 1.3 %collective-permute-start.1 = (f32[4,64,128]{2,1,0:T(8,128)S(1)}, f32[4,64,128]{2,1,0:T(8,128)S(1)}, u32[]{:S(2)}, u32[]{:S(2)}) collective-permute-start(f32[4,64,128]{2,1,0:T(8,128)S(1)} %get-tuple-element.215), channel_id=1, source_target_pairs={{1,0},{2,1},{3,2},{4,3},{5,4},{6,5},{7,6},{8,7},{9,8},{10,9},{11,1... | collective-permute-start | bytes 393224 | tf_op jit(solution)/shard_map/ppermute | solution.py:21
  3.1 3.0 %collective-permute-start = (f32[4,64,128]{2,1,0:T(8,128)S(1)}, f32[4,64,128]{2,1,0:T(8,128)S(1)}, u32[]{:S(2)}, u32[]{:S(2)}) collective-permute-start(f32[4,64,128]{2,1,0:T(8,128)S(1)} %get-tuple-element.214), channel_id=1, source_target_pairs={{0,1},{1,2},{2,3},{3,4},{4,5},{5,6},{6,7},{7,8},{8,9},{9,10},{10,1... | collective-permute-start | bytes 393224 | tf_op jit(solution)/shard_map/ppermute | solution.py:18
  6.2 1.0 constant_dynamic-update-slice_fusion.1
  9.5 8.7 %copy.264 = f32[3,256,128]{0,2,1:T(8,128)} copy(f32[3,256,128]{2,1,0:T(8,128)S(1)} %copy-done) | data formatting | bytes 786432 | tf_op args[0]
  18.3 6.4 %gather_fusion.9 = f32[128,3]{1,0:T(8,128)S(1)} fusion(f32[3,32768]{0,1:T(8,128)} %bitcast.171, s32[1024]{0:T(1024)S(1)} %pad_clamp_fusion), kind=kCustom, calls=%fused_computation.12 | custom fusion | bytes 3584 | tf_op jit(solution)/shard_map/gather | solution.py:168
  24.7 1.2 %gather_fusion.10 = f32[128]{0:T(128)S(1)} fusion(f32[32768]{0:T(1024)S(1)} %bitcast.174, s32[1024]{0:T(1024)S(1)} %pad_clamp_fusion), kind=kCustom, calls=%fused_computation.13 | custom fusion | bytes 1536 | tf_op jit(solution)/shard_map/gather | solution.py:169
  25.9 1.1 %gather_fusion.11 = f32[128]{0:T(128)S(1)} fusion(f32[32768]{0:T(1024)S(1)} %bitcast.177, s32[1024]{0:T(1024)S(1)} %pad_clamp_fusion), kind=kCustom, calls=%fused_computation.14 | custom fusion | bytes 1536 | tf_op jit(solution)/shard_map/gather | solution.py:170
  27.1 1.1 %gather_fusion.12 = f32[128]{0:T(128)S(1)} fusion(f32[32768]{0:T(1024)S(1)} %bitcast.178, s32[1024]{0:T(1024)S(1)} %pad_clamp_fusion), kind=kCustom, calls=%fused_computation.15 | custom fusion | bytes 1536 | tf_op jit(solution)/shard_map/gather | solution.py:171
  28.3 0.6 gather_fusion
  29.4 0.7 gather_fusion.14
  30.2 9.0 %while.20 = (s32[]{:T(128)}, f32[4,128]{1,0:T(4,128)S(1)}, f32[4,27,128]{2,1,0:T(8,128)S(1)}, f32[4,3,128]{2,1,0:T(4,128)S(1)}, f32[4,3,27,128]{3,2,0,1:T(8,128)...) while((s32[]{:T(128)}, f32[4,128]{1,0:T(4,128)S(1)}, f32[4,27,128]{2,1,0:T(8,128)S(1)}, ...), condition=%wide.region_3.5_spmd, body=%wide.region_0.4_spmd.sunk | while | flops 10617218 | bytes 3714165 | solution.py:106
  30.3 0.7 multiply_reduce_fusion.2
  31.0 1.4 %fusion.42 = f32[128]{0:T(128)S(1)} fusion(f32[128,27,128]{2,0,1:T(8,128)S(1)} %multiply_reduce_fusion.2, f32[128]{0:T(128)S(1)} %fusion.41, f32[27,128]{1,0:T(8,128)S(1)} %dynamic-slice_bitcast_fusion.12), kind=kLoop, calls=%fused_computation.27.clone.1 | loop fusion | flops 7077760 | bytes 1784320 | tf_op jit(solution)/shard_map/while/body/eval_jaxpr/reduce_sum | solution.py:53
  32.5 0.7 multiply_reduce_fusion.2
  33.3 1.4 %fusion.42 = f32[128]{0:T(128)S(1)} fusion(f32[128,27,128]{2,0,1:T(8,128)S(1)} %multiply_reduce_fusion.2, f32[128]{0:T(128)S(1)} %fusion.41, f32[27,128]{1,0:T(8,128)S(1)} %dynamic-slice_bitcast_fusion.12), kind=kLoop, calls=%fused_computation.27.clone.1 | loop fusion | flops 7077760 | bytes 1784320 | tf_op jit(solution)/shard_map/while/body/eval_jaxpr/reduce_sum | solution.py:53
  34.8 0.7 multiply_reduce_fusion.2
  35.5 1.4 %fusion.42 = f32[128]{0:T(128)S(1)} fusion(f32[128,27,128]{2,0,1:T(8,128)S(1)} %multiply_reduce_fusion.2, f32[128]{0:T(128)S(1)} %fusion.41, f32[27,128]{1,0:T(8,128)S(1)} %dynamic-slice_bitcast_fusion.12), kind=kLoop, calls=%fused_computation.27.clone.1 | loop fusion | flops 7077760 | bytes 1784320 | tf_op jit(solution)/shard_map/while/body/eval_jaxpr/reduce_sum | solution.py:53
  37.1 0.7 multiply_reduce_fusion.2
  37.8 1.4 %fusion.42 = f32[128]{0:T(128)S(1)} fusion(f32[128,27,128]{2,0,1:T(8,128)S(1)} %multiply_reduce_fusion.2, f32[128]{0:T(128)S(1)} %fusion.41, f32[27,128]{1,0:T(8,128)S(1)} %dynamic-slice_bitcast_fusion.12), kind=kLoop, calls=%fused_computation.27.clone.1 | loop fusion | flops 7077760 | bytes 1784320 | tf_op jit(solution)/shard_map/while/body/eval_jaxpr/reduce_sum | solution.py:53
  39.3 0.7 scatter_custom_fusion
  40.0 1.1 %gather_fusion.13 = f32[128]{0:T(128)S(1)} fusion(f32[32768]{0:T(1024)S(1)} %bitcast.172, s32[1024]{0:T(1024)S(1)} %pad_clamp_fusion), kind=kCustom, calls=%fused_computation.16 | custom fusion | bytes 1536 | tf_op jit(solution)/shard_map/gather | solution.py:172
  41.3 0.9 scatter_custom_fusion.1
  42.4 1.3 %collective-permute-start.3 = (f32[7,64,128]{2,1,0:T(8,128)S(1)}, f32[7,64,128]{2,1,0:T(8,128)S(1)}, u32[]{:S(2)}, u32[]{:S(2)}) collective-permute-start(f32[7,64,128]{2,1,0:T(8,128)S(1)} %get-tuple-element.213), channel_id=1, source_target_pairs={{1,0},{2,1},{3,2},{4,3},{5,4},{6,5},{7,6},{8,7},{9,8},{10,9},{11,1... | collective-permute-start | bytes 688136 | tf_op jit(solution)/shard_map/ppermute | solution.py:21
  43.7 5.1 %collective-permute-start.2 = (f32[7,64,128]{2,1,0:T(8,128)S(1)}, f32[7,64,128]{2,1,0:T(8,128)S(1)}, u32[]{:S(2)}, u32[]{:S(2)}) collective-permute-start(f32[7,64,128]{2,1,0:T(8,128)S(1)} %get-tuple-element.212), channel_id=1, source_target_pairs={{0,1},{1,2},{2,3},{3,4},{4,5},{5,6},{6,7},{7,8},{8,9},{9,10},{10,1... | collective-permute-start | bytes 688136 | tf_op jit(solution)/shard_map/ppermute | solution.py:18
  63.3 0.6 constant_dynamic-update-slice_fusion.13
  70.3 9.9 %all-to-all-start = ((f32[32,7,8]{2,1,0:T(8,128)}), f32[32,7,8]{2,1,0:T(8,128)S(1)}, u32[]{:S(2)}, u32[]{:S(2)}) async-start(f32[32,7,8]{2,1,0:T(8,128)} %constant_dynamic-update-slice_fusion.2), calls=%async_computation | async-start | bytes 262144 | tf_op jit(solution)/shard_map/all_to_all | solution.py:183
  81.4 6.9 %all-to-all-done = f32[32,7,8]{2,1,0:T(8,128)S(1)} async-done(((f32[32,7,8]{2,1,0:T(8,128)}), f32[32,7,8]{2,1,0:T(8,128)S(1)}, u32[]{:S(2)}, u32[]{:S(2)}) %all-to-all-start) | async-done | bytes 7200 | tf_op jit(solution)/shard_map/all_to_all | solution.py:183
  88.3 0.7 reshape.260
  89.1 0.6 gather_fusion.3
  90.3 0.7 gather_fusion.15
  91.1 0.6 gather_fusion.6
  91.8 0.6 gather_fusion.7
  92.4 0.6 gather_fusion.8
  93.1 14.6 %while.21 = (s32[]{:T(128)}, f32[4,3,128]{2,0,1:T(4,128)S(1)}, f32[4,27,128]{2,1,0:T(8,128)S(1)}, f32[4,128]{1,0:T(4,128)S(1)}, f32[4,128]{1,0:T(4,128)S(1)}, /*...) while((s32[]{:T(128)}, f32[4,3,128]{2,0,1:T(4,128)S(1)}, ...), condition=%wide.region_8.10_spmd, body=%wide.region_5.9_spmd.sunk | while | flops 19931648 | bytes 7402649 | solution.py:146
  93.1 0.7 fusion.45
  93.8 2.1 %add_multiply_fusion.2 = f32[128,27,128]{2,0,1:T(8,128)S(1)} fusion(f32[128,27,128]{2,0,1:T(8,128)S(1)} %fusion.45, f32[27,128]{1,0:T(8,128)S(1)} %get-tuple-element.361, f32[27,128]{1,0:T(8,128)S(1)} %get-tuple-element.362, f32[128]{0:T(128)S(1)} %get-tuple-element.363, f32[128]{0:T(128)S(1)} %get-tuple-element.364, f32[27,128]{1,0:T(8,128)S(1)} %get-tuple-element.365), kind=kLoop, calls=%fused_computation.42.clone.1 | loop fusion | flops 12386304 | bytes 3581440 | tf_op jit(solution)/shard_map/while/body/eval_jaxpr/mul | solution.py:66
  96.0 0.7 fusion.46
  96.8 0.7 fusion.45
  97.5 2.1 %add_multiply_fusion.2 = f32[128,27,128]{2,0,1:T(8,128)S(1)} fusion(f32[128,27,128]{2,0,1:T(8,128)S(1)} %fusion.45, f32[27,128]{1,0:T(8,128)S(1)} %get-tuple-element.361, f32[27,128]{1,0:T(8,128)S(1)} %get-tuple-element.362, f32[128]{0:T(128)S(1)} %get-tuple-element.363, f32[128]{0:T(128)S(1)} %get-tuple-element.364, f32[27,128]{1,0:T(8,128)S(1)} %get-tuple-element.365), kind=kLoop, calls=%fused_computation.42.clone.1 | loop fusion | flops 12386304 | bytes 3581440 | tf_op jit(solution)/shard_map/while/body/eval_jaxpr/mul | solution.py:66
  99.6 0.7 fusion.46
  100.4 0.7 fusion.45
  101.1 2.1 %add_multiply_fusion.2 = f32[128,27,128]{2,0,1:T(8,128)S(1)} fusion(f32[128,27,128]{2,0,1:T(8,128)S(1)} %fusion.45, f32[27,128]{1,0:T(8,128)S(1)} %get-tuple-element.361, f32[27,128]{1,0:T(8,128)S(1)} %get-tuple-element.362, f32[128]{0:T(128)S(1)} %get-tuple-element.363, f32[128]{0:T(128)S(1)} %get-tuple-element.364, f32[27,128]{1,0:T(8,128)S(1)} %get-tuple-element.365), kind=kLoop, calls=%fused_computation.42.clone.1 | loop fusion | flops 12386304 | bytes 3581440 | tf_op jit(solution)/shard_map/while/body/eval_jaxpr/mul | solution.py:66
  103.3 0.7 fusion.46
  104.1 0.7 fusion.45
  104.8 2.1 %add_multiply_fusion.2 = f32[128,27,128]{2,0,1:T(8,128)S(1)} fusion(f32[128,27,128]{2,0,1:T(8,128)S(1)} %fusion.45, f32[27,128]{1,0:T(8,128)S(1)} %get-tuple-element.361, f32[27,128]{1,0:T(8,128)S(1)} %get-tuple-element.362, f32[128]{0:T(128)S(1)} %get-tuple-element.363, f32[128]{0:T(128)S(1)} %get-tuple-element.364, f32[27,128]{1,0:T(8,128)S(1)} %get-tuple-element.365), kind=kLoop, calls=%fused_computation.42.clone.1 | loop fusion | flops 12386304 | bytes 3581440 | tf_op jit(solution)/shard_map/while/body/eval_jaxpr/mul | solution.py:66
  106.9 0.7 fusion.46
  107.7 0.7 multiply_bitcast_fusion
  (185 shorter events, 26.1 us)
Async XLA Ops:
  0.6 6.7 %copy-start = (f32[3,256,128]{2,1,0:T(8,128)S(1)}, f32[3,256,128]{2,1,0:T(8,128)}, u32[]{:S(2)}) copy-start(f32[3,256,128]{2,1,0:T(8,128)} %param.16) | copy-start | bytes 1179652
  0.6 8.0 %copy-start.3 = (f32[256,128]{1,0:T(8,128)S(1)}, f32[256,128]{1,0:T(8,128)}, u32[]{:S(2)}) copy-start(f32[256,128]{1,0:T(8,128)} %param.17) | copy-start | bytes 393220
  0.7 8.3 %copy-start.4 = (f32[256,128]{1,0:T(8,128)S(1)}, f32[256,128]{1,0:T(8,128)}, u32[]{:S(2)}) copy-start(f32[256,128]{1,0:T(8,128)} %param.18) | copy-start | bytes 393220
  0.7 6.6 %copy-start.7 = (s32[4]{0:T(128)S(1)}, s32[4]{0:T(128)}, u32[]{:S(2)}) copy-start(s32[4]{0:T(128)} %param.21) | copy-start | bytes 52
  0.7 6.6 %copy-start.6 = (s32[4,27]{1,0:T(4,128)S(1)}, s32[4,27]{1,0:T(4,128)}, u32[]{:S(2)}) copy-start(s32[4,27]{1,0:T(4,128)} %param.23) | copy-start | bytes 1300
  0.7 8.1 %copy-start.9 = (s32[128]{0:T(128)S(1)}, s32[128]{0:T(128)}, u32[]{:S(2)}) copy-start(s32[128]{0:T(128)} %param.24) | copy-start | bytes 1540
  0.7 7.9 %copy-start.8 = (s32[128,1]{0,1:T(1,128)S(1)}, s32[128,1]{0,1:T(1,128)}, u32[]{:S(2)}) copy-start(s32[128,1]{0,1:T(1,128)} %param.25) | copy-start | bytes 1540
  1.8 26.4 %collective-permute-start.1 = (f32[4,64,128]{2,1,0:T(8,128)S(1)}, f32[4,64,128]{2,1,0:T(8,128)S(1)}, u32[]{:S(2)}, u32[]{:S(2)}) collective-permute-start(f32[4,64,128]{2,1,0:T(8,128)S(1)} %get-tuple-element.215), channel_id=1, source_target_pairs={{1,0},{2,1},{3,2},{4,3},{5,4},{6,5},{7,6},{8,7},{9,8},{10,9},{11,1... | collective-permute-start | bytes 393224 | tf_op jit(solution)/shard_map/ppermute | solution.py:21
  3.1 25.2 %collective-permute-start = (f32[4,64,128]{2,1,0:T(8,128)S(1)}, f32[4,64,128]{2,1,0:T(8,128)S(1)}, u32[]{:S(2)}, u32[]{:S(2)}) collective-permute-start(f32[4,64,128]{2,1,0:T(8,128)S(1)} %get-tuple-element.214), channel_id=1, source_target_pairs={{0,1},{1,2},{2,3},{3,4},{4,5},{5,6},{6,7},{7,8},{8,9},{9,10},{10,1... | collective-permute-start | bytes 393224 | tf_op jit(solution)/shard_map/ppermute | solution.py:18
  9.5 17.5 %copy-start.5 = (f32[256,128]{1,0:T(8,128)S(1)}, f32[256,128]{1,0:T(8,128)}, u32[]{:S(2)}) copy-start(f32[256,128]{1,0:T(8,128)} %param.19) | copy-start | bytes 393220
  30.2 9.0 %copy-start.2 = (f32[256,128]{1,0:T(8,128)S(1)}, f32[256,128]{1,0:T(8,128)}, u32[]{:S(2)}) copy-start(f32[256,128]{1,0:T(8,128)} %param.20) | copy-start | bytes 393220
  40.0 40.3 %copy-start.1 = (f32[256,128]{1,0:T(8,128)}, f32[256,128]{1,0:T(8,128)S(1)}, u32[]{:S(2)}) copy-start(f32[256,128]{1,0:T(8,128)S(1)} %scatter_custom_fusion) | copy-start | bytes 393220
  42.4 46.6 %collective-permute-start.3 = (f32[7,64,128]{2,1,0:T(8,128)S(1)}, f32[7,64,128]{2,1,0:T(8,128)S(1)}, u32[]{:S(2)}, u32[]{:S(2)}) collective-permute-start(f32[7,64,128]{2,1,0:T(8,128)S(1)} %get-tuple-element.213), channel_id=1, source_target_pairs={{1,0},{2,1},{3,2},{4,3},{5,4},{6,5},{7,6},{8,7},{9,8},{10,9},{11,1... | collective-permute-start | bytes 688136 | tf_op jit(solution)/shard_map/ppermute | solution.py:21
  43.7 45.3 %collective-permute-start.2 = (f32[7,64,128]{2,1,0:T(8,128)S(1)}, f32[7,64,128]{2,1,0:T(8,128)S(1)}, u32[]{:S(2)}, u32[]{:S(2)}) collective-permute-start(f32[7,64,128]{2,1,0:T(8,128)S(1)} %get-tuple-element.212), channel_id=1, source_target_pairs={{0,1},{1,2},{2,3},{3,4},{4,5},{5,6},{6,7},{7,8},{8,9},{9,10},{10,1... | collective-permute-start | bytes 688136 | tf_op jit(solution)/shard_map/ppermute | solution.py:18
  70.3 17.9 %all-to-all-start = ((f32[32,7,8]{2,1,0:T(8,128)}), f32[32,7,8]{2,1,0:T(8,128)S(1)}, u32[]{:S(2)}, u32[]{:S(2)}) async-start(f32[32,7,8]{2,1,0:T(8,128)} %constant_dynamic-update-slice_fusion.2), calls=%async_computation | async-start | bytes 262144 | tf_op jit(solution)/shard_map/all_to_all | solution.py:183
